TPU v7x, 32 devices: a whole 2x2x4 slice. The times are simulated.
32 devices in a mesh: fsdp: 8 (over z, x), dp: 4 (over y, core).
Axes of the slice: x: 2, y: 2, z: 4, core: 2. Of those that a mesh axis runs over, the one named last changes fastest.
Arguments:
- inputs: bfloat16 [18464, 1024], P(('fsdp', 'dp')), may hold values from -6 to 6
- cotangent: bfloat16 [18464, 1024], P(('fsdp', 'dp')), may hold values from -6 to 6
- norm1_gain: float32 [1024], P('fsdp'), may hold values from 0.08 to 2.5
- norm1_bias: float32 [1024], P('fsdp'), may hold values from -1.2 to 1.2
- qkv_weight: float32 [1024, 3072], P('fsdp'), may hold values from -0.1875 to 0.1875
- qv_bias: float32 [2048], P('fsdp'), may hold values from -3 to 3
- out_weight: float32 [1024, 1024], P('fsdp'), may hold values from -3 to 3
- out_bias: float32 [1024], P('fsdp'), may hold values from -3 to 3
- norm2_gain: float32 [1024], P('fsdp'), may hold values from 0.08 to 2.5
- norm2_bias: float32 [1024], P('fsdp'), may hold values from -1.2 to 1.2
- in_weight: float32 [1024, 4096], P('fsdp'), may hold values from -0.1875 to 0.1875
- in_bias: float32 [4096], P('fsdp'), may hold values from -3 to 3
- down_weight: float32 [4096, 1024], P('fsdp'), may hold values from -0.09375 to 0.09375
- down_bias: float32 [1024], P('fsdp'), may hold values from -3 to 3
- qkv_rows: float32 [1024], P('fsdp'), may hold values from 0.34375 to 196.875
- qkv_cols: float32 [3072], replicated, may hold values from 0.9375 to 93.75
- out_rows: float32 [1024], P('fsdp'), may hold values from 0.003125 to 2.8125
- out_cols: float32 [1024], replicated, may hold values from 0.009375 to 0.9375
- in_rows: float32 [1024], P('fsdp'), may hold values from 0.05625 to 31.5625
- in_cols: float32 [4096], replicated, may hold values from 0.15625 to 15.625
- down_rows: float32 [4096], P('fsdp'), may hold values from 0.20833333 to 187.5
- down_cols: float32 [1024], replicated, may hold values from 0.625 to 62.5
- norm1_gain_moment: float32 [1024], P('fsdp'), may hold values from 0.104166667 to 281.25
- norm1_bias_moment: float32 [1024], P('fsdp'), may hold values from 0.104166667 to 281.25
- qv_bias_moment: float32 [2048], P('fsdp'), may hold values from 0.104166667 to 281.25
- out_bias_moment: float32 [1024], P('fsdp'), may hold values from 0.104166667 to 281.25
- norm2_gain_moment: float32 [1024], P('fsdp'), may hold values from 0.104166667 to 281.25
- norm2_bias_moment: float32 [1024], P('fsdp'), may hold values from 0.104166667 to 281.25
- in_bias_moment: float32 [4096], P('fsdp'), may hold values from 0.104166667 to 281.25
- down_bias_moment: float32 [1024], P('fsdp'), may hold values from 0.104166667 to 281.25
Outputs:
- output: bfloat16 [18464, 1024], P(('fsdp', 'dp'))
- input_grad: bfloat16 [18464, 1024], P(('fsdp', 'dp'))
- grad_norm1_gain: float32 [1024], P('fsdp')
- grad_norm1_bias: float32 [1024], P('fsdp')
- grad_qkv_weight: float32 [1024, 3072], P('fsdp')
- grad_qv_bias: float32 [2048], P('fsdp')
- grad_out_weight: float32 [1024, 1024], P('fsdp')
- grad_out_bias: float32 [1024], P('fsdp')
- grad_norm2_gain: float32 [1024], P('fsdp')
- grad_norm2_bias: float32 [1024], P('fsdp')
- grad_in_weight: float32 [1024, 4096], P('fsdp')
- grad_in_bias: float32 [4096], P('fsdp')
- grad_down_weight: float32 [4096, 1024], P('fsdp')
- grad_down_bias: float32 [1024], P('fsdp')
- new_qkv_rows: float32 [1024], P('fsdp')
- new_qkv_cols: float32 [3072], replicated
- new_out_rows: float32 [1024], P('fsdp')
- new_out_cols: float32 [1024], replicated
- new_in_rows: float32 [1024], P('fsdp')
- new_in_cols: float32 [4096], replicated
- new_down_rows: float32 [4096], P('fsdp')
- new_down_cols: float32 [1024], replicated
- new_norm1_gain_moment: float32 [1024], P('fsdp')
- new_norm1_bias_moment: float32 [1024], P('fsdp')
- new_qv_bias_moment: float32 [2048], P('fsdp')
- new_out_bias_moment: float32 [1024], P('fsdp')
- new_norm2_gain_moment: float32 [1024], P('fsdp')
- new_norm2_bias_moment: float32 [1024], P('fsdp')
- new_in_bias_moment: float32 [4096], P('fsdp')
- new_down_bias_moment: float32 [1024], P('fsdp')
- new_norm1_gain: float32 [1024], P('fsdp')
- new_norm1_bias: float32 [1024], P('fsdp')
- new_qkv_weight: float32 [1024, 3072], P('fsdp')
- new_qv_bias: float32 [2048], P('fsdp')
- new_out_weight: float32 [1024, 1024], P('fsdp')
- new_out_bias: float32 [1024], P('fsdp')
- new_norm2_gain: float32 [1024], P('fsdp')
- new_norm2_bias: float32 [1024], P('fsdp')
- new_in_weight: float32 [1024, 4096], P('fsdp')
- new_in_bias: float32 [4096], P('fsdp')
- new_down_weight: float32 [4096, 1024], P('fsdp')
- new_down_bias: float32 [1024], P('fsdp')
- clip_factors: float32 [12], replicated
All inputs are finite; a program needn't handle non-finite values.
Results may differ from a plain program's by a relative error of at most 0.01.
The roundings to bfloat16 on the way count: a program that leaves them out, or rounds other values in their place, can miss the bound.
Values may be sent and summed in bfloat16 or wider, within the bound.
No kernel may reach another device: no remote copies, remote signals or barrier semaphores. Data moves between devices by JAX's collectives and lax.ppermute only.
A program may use at most 256 MiB of HBM per device.

v0:
```python
import math
import jax
import jax.numpy as jnp
from jax import lax
from jax.sharding import PartitionSpec as P

HEAD_DIM = 64
SEQ = 577
ln_eps = 1e-06
clip_level = 0.05
step_rate = 4.0


def norm_rows(values):
    centre = values - jnp.mean(values, axis=-1, keepdims=True)
    spread = jnp.mean(centre * centre, axis=-1, keepdims=True)
    return centre * lax.rsqrt(spread + ln_eps)


def norm_affine(values, gain_full, bias_full):
    return norm_rows(values) * gain_full + bias_full


def gelu_exact(values):
    return jax.nn.gelu(values, approximate=False)


def plain_dot(left, right):
    return jnp.dot(left, right, preferred_element_type=jnp.float32)


def lead_dot(left, right):
    return lax.dot_general(
        left, right, (((0,), (0,)), ((), ())), preferred_element_type=jnp.float32
    )


def tail_dot(left, right):
    return lax.dot_general(
        left, right, (((1,), (1,)), ((), ())), preferred_element_type=jnp.float32
    )


def split_heads(rows):
    return rows.reshape(rows.shape[0], rows.shape[1] // HEAD_DIM, HEAD_DIM)


def attend(block):
    query_rows, key_rows, value_rows = block
    length, width = query_rows.shape
    scale = 1.0 / math.sqrt(HEAD_DIM)
    scores = (
        jnp.einsum(
            "qhd,khd->hqk",
            split_heads(query_rows),
            split_heads(key_rows),
            preferred_element_type=jnp.float32,
        )
        * scale
    )
    highest = jnp.max(scores, axis=-1, keepdims=True)
    exponent = jnp.exp(scores - highest)
    summed = jnp.sum(exponent, axis=-1, keepdims=True)
    probs = exponent / summed
    mixed = jnp.einsum(
        "hqk,khd->qhd",
        probs.astype(jnp.bfloat16),
        split_heads(value_rows),
        preferred_element_type=jnp.float32,
    )
    logsum = (highest + jnp.log(summed))[..., 0]
    return (mixed.reshape(length, width).astype(jnp.bfloat16), logsum)


def attend_back(block):
    query_rows, key_rows, value_rows, logsum, grad_rows = block
    length, width = query_rows.shape
    scale = 1.0 / math.sqrt(HEAD_DIM)
    query_h = split_heads(query_rows)
    key_h = split_heads(key_rows)
    value_h = split_heads(value_rows)
    grad_h = split_heads(grad_rows)
    scores = jnp.einsum("qhd,khd->hqk", query_h, key_h, preferred_element_type=jnp.float32) * scale
    probs = jnp.exp(scores - logsum[..., None])
    grad_probs = jnp.einsum("qhd,khd->hqk", grad_h, value_h, preferred_element_type=jnp.float32)
    grad_value = jnp.einsum(
        "hqk,qhd->khd", probs.astype(jnp.bfloat16), grad_h, preferred_element_type=jnp.float32
    )
    inner = jnp.sum(probs * grad_probs, axis=-1, keepdims=True)
    grad_scores = (probs * (grad_probs - inner)).astype(jnp.bfloat16) * jnp.asarray(
        scale, jnp.bfloat16
    )
    grad_query = jnp.einsum("hqk,khd->qhd", grad_scores, key_h, preferred_element_type=jnp.float32)
    grad_key = jnp.einsum("hqk,qhd->khd", grad_scores, query_h, preferred_element_type=jnp.float32)
    joined = jnp.concatenate(
        [
            grad_query.reshape(length, width),
            grad_key.reshape(length, width),
            grad_value.reshape(length, width),
        ],
        axis=1,
    )
    return joined.astype(jnp.bfloat16)


def on_device(
    inputs,
    cotangent,
    norm1_gain,
    norm1_bias,
    qkv_weight,
    qv_bias,
    out_weight,
    out_bias,
    norm2_gain,
    norm2_bias,
    in_weight,
    in_bias,
    down_weight,
    down_bias,
    qkv_rows,
    qkv_cols,
    out_rows,
    out_cols,
    in_rows,
    in_cols,
    down_rows,
    down_cols,
    norm1_gain_moment,
    norm1_bias_moment,
    qv_bias_moment,
    out_bias_moment,
    norm2_gain_moment,
    norm2_bias_moment,
    in_bias_moment,
    down_bias_moment,
):
    masters = [
        norm1_gain,
        norm1_bias,
        qkv_weight,
        qv_bias,
        out_weight,
        out_bias,
        norm2_gain,
        norm2_bias,
        in_weight,
        in_bias,
        down_weight,
        down_bias,
    ]
    halves = [member.astype(jnp.bfloat16) for member in masters]
    gathered = (
        lax.all_gather(halves[0], "fsdp", axis=0, tiled=True),
        lax.all_gather(halves[1], "fsdp", axis=0, tiled=True),
        lax.all_gather(halves[2], "fsdp", axis=0, tiled=True),
        lax.all_gather(halves[3], "fsdp", axis=0, tiled=True),
        lax.all_gather(halves[4], "fsdp", axis=0, tiled=True),
        lax.all_gather(halves[5], "fsdp", axis=0, tiled=True),
        lax.all_gather(halves[6], "fsdp", axis=0, tiled=True),
        lax.all_gather(halves[7], "fsdp", axis=0, tiled=True),
        lax.all_gather(halves[8], "fsdp", axis=0, tiled=True),
        lax.all_gather(halves[9], "fsdp", axis=0, tiled=True),
        lax.all_gather(halves[10], "fsdp", axis=0, tiled=True),
        lax.all_gather(halves[11], "fsdp", axis=0, tiled=True),
    )
    (
        gain_one,
        bias_one,
        weight_qkv,
        bias_qv,
        weight_out,
        bias_out,
        gain_two,
        bias_two,
        weight_in,
        bias_in,
        weight_down,
        bias_down,
    ) = gathered
    tokens, width = inputs.shape
    images = tokens // SEQ
    rows_in = inputs.astype(jnp.float32)
    normed_f, pull_one = jax.vjp(
        norm_affine, rows_in, gain_one.astype(jnp.float32), bias_one.astype(jnp.float32)
    )
    normed = normed_f.astype(jnp.bfloat16)
    qkv = plain_dot(normed, weight_qkv)
    bias_pair = bias_qv.astype(jnp.float32)
    query = (qkv[:, :width] + bias_pair[:width]).astype(jnp.bfloat16)
    keys = qkv[:, width : 2 * width].astype(jnp.bfloat16)
    values = (qkv[:, 2 * width :] + bias_pair[width:]).astype(jnp.bfloat16)
    query_img = query.reshape(images, SEQ, width)
    keys_img = keys.reshape(images, SEQ, width)
    values_img = values.reshape(images, SEQ, width)
    attended_img, logsum = lax.map(attend, (query_img, keys_img, values_img))
    attended = attended_img.reshape(tokens, width)
    middle = rows_in + plain_dot(attended, weight_out) + bias_out.astype(jnp.float32)
    normed_mid_f, pull_two = jax.vjp(
        norm_affine, middle, gain_two.astype(jnp.float32), bias_two.astype(jnp.float32)
    )
    normed_mid = normed_mid_f.astype(jnp.bfloat16)
    preact = plain_dot(normed_mid, weight_in) + bias_in.astype(jnp.float32)
    hidden_f, pull_gelu = jax.vjp(gelu_exact, preact)
    hidden = hidden_f.astype(jnp.bfloat16)
    final = middle + plain_dot(hidden, weight_down) + bias_down.astype(jnp.float32)
    output = final.astype(jnp.bfloat16)
    grad_out_rows = cotangent.astype(jnp.float32)
    term_down_weight = lead_dot(hidden, cotangent)
    term_down_bias = jnp.sum(grad_out_rows, axis=0)
    grad_hidden = tail_dot(cotangent, weight_down)
    (grad_preact,) = pull_gelu(grad_hidden)
    grad_preact_low = grad_preact.astype(jnp.bfloat16)
    term_in_weight = lead_dot(normed_mid, grad_preact_low)
    term_in_bias = jnp.sum(grad_preact_low.astype(jnp.float32), axis=0)
    grad_normed_mid = tail_dot(grad_preact_low, weight_in)
    grad_mid_norm, term_gain_two, term_bias_two = pull_two(grad_normed_mid)
    grad_mid = grad_out_rows + grad_mid_norm
    grad_mid_low = grad_mid.astype(jnp.bfloat16)
    term_out_weight = lead_dot(attended, grad_mid_low)
    term_out_bias = jnp.sum(grad_mid_low.astype(jnp.float32), axis=0)
    grad_attended = tail_dot(grad_mid_low, weight_out).astype(jnp.bfloat16)
    grad_qkv_img = lax.map(
        attend_back,
        (query_img, keys_img, values_img, logsum, grad_attended.reshape(images, SEQ, width)),
    )
    grad_qkv = grad_qkv_img.reshape(tokens, 3 * width)
    term_qkv_weight = lead_dot(normed, grad_qkv)
    column_sums = jnp.sum(grad_qkv.astype(jnp.float32), axis=0)
    term_qv_bias = jnp.concatenate([column_sums[:width], column_sums[2 * width :]])
    grad_normed = tail_dot(grad_qkv, weight_qkv)
    grad_in_norm, term_gain_one, term_bias_one = pull_one(grad_normed)
    input_grad = (grad_mid + grad_in_norm).astype(jnp.bfloat16)
    terms = [
        term_gain_one,
        term_bias_one,
        term_qkv_weight,
        term_qv_bias,
        term_out_weight,
        term_out_bias,
        term_gain_two,
        term_bias_two,
        term_in_weight,
        term_in_bias,
        term_down_weight,
        term_down_bias,
    ]
    pieces = (
        lax.psum_scatter(terms[0], ("fsdp", "dp"), scatter_dimension=0, tiled=True),
        lax.psum_scatter(terms[1], ("fsdp", "dp"), scatter_dimension=0, tiled=True),
        lax.psum_scatter(terms[2], ("fsdp", "dp"), scatter_dimension=0, tiled=True),
        lax.psum_scatter(terms[3], ("fsdp", "dp"), scatter_dimension=0, tiled=True),
        lax.psum_scatter(terms[4], ("fsdp", "dp"), scatter_dimension=0, tiled=True),
        lax.psum_scatter(terms[5], ("fsdp", "dp"), scatter_dimension=0, tiled=True),
        lax.psum_scatter(terms[6], ("fsdp", "dp"), scatter_dimension=0, tiled=True),
        lax.psum_scatter(terms[7], ("fsdp", "dp"), scatter_dimension=0, tiled=True),
        lax.psum_scatter(terms[8], ("fsdp", "dp"), scatter_dimension=0, tiled=True),
        lax.psum_scatter(terms[9], ("fsdp", "dp"), scatter_dimension=0, tiled=True),
        lax.psum_scatter(terms[10], ("fsdp", "dp"), scatter_dimension=0, tiled=True),
        lax.psum_scatter(terms[11], ("fsdp", "dp"), scatter_dimension=0, tiled=True),
    )
    shards = (
        lax.all_gather(pieces[0], "dp", axis=0, tiled=True),
        lax.all_gather(pieces[1], "dp", axis=0, tiled=True),
        lax.all_gather(pieces[2], "dp", axis=0, tiled=True),
        lax.all_gather(pieces[3], "dp", axis=0, tiled=True),
        lax.all_gather(pieces[4], "dp", axis=0, tiled=True),
        lax.all_gather(pieces[5], "dp", axis=0, tiled=True),
        lax.all_gather(pieces[6], "dp", axis=0, tiled=True),
        lax.all_gather(pieces[7], "dp", axis=0, tiled=True),
        lax.all_gather(pieces[8], "dp", axis=0, tiled=True),
        lax.all_gather(pieces[9], "dp", axis=0, tiled=True),
        lax.all_gather(pieces[10], "dp", axis=0, tiled=True),
        lax.all_gather(pieces[11], "dp", axis=0, tiled=True),
    )
    group_size = lax.axis_size("fsdp")
    images_all = images * group_size * lax.axis_size("dp")
    grads = [member / images_all for member in shards]
    row_states = [qkv_rows, out_rows, in_rows, down_rows]
    col_states = [qkv_cols, out_cols, in_cols, down_cols]
    moments = [
        norm1_gain_moment,
        norm1_bias_moment,
        qv_bias_moment,
        out_bias_moment,
        norm2_gain_moment,
        norm2_bias_moment,
        in_bias_moment,
        down_bias_moment,
    ]
    matrix_slots = {2: 0, 4: 1, 8: 2, 10: 3}
    vector_slots = {0: 0, 1: 1, 3: 2, 5: 3, 6: 4, 7: 5, 9: 6, 11: 7}
    prepared = []
    packs = []
    for number in range(12):
        weight = masters[number]
        squared = grads[number] * grads[number]
        if number in matrix_slots:
            position = matrix_slots[number]
            new_rows = 0.5 * row_states[position] + 0.5 * jnp.mean(squared, axis=1)
            prepared.append(new_rows)
            packs.append(
                jnp.concatenate(
                    [
                        jnp.sum(squared, axis=0),
                        jnp.stack([jnp.sum(new_rows), jnp.sum(weight * weight)]),
                    ]
                )
            )
        else:
            position = vector_slots[number]
            prepared.append(0.5 * moments[position] + 0.5 * squared)
            packs.append(jnp.sum(weight * weight).reshape(1))
    totals = [lax.psum(packed, "fsdp") for packed in packs]
    directions = []
    counts = []
    weight_sums = []
    direction_sums = []
    new_cols_all = [None] * 4
    for number in range(12):
        weight = masters[number]
        grad = grads[number]
        if number in matrix_slots:
            position = matrix_slots[number]
            rows_total = weight.shape[0] * group_size
            new_cols = 0.5 * col_states[position] + 0.5 * totals[number][:-2] / rows_total
            new_cols_all[position] = new_cols
            mean_rows = totals[number][-2] / rows_total
            estimate = prepared[number][:, None] * new_cols[None, :] / mean_rows
            direction = grad * lax.rsqrt(estimate)
            counts.append(rows_total * weight.shape[1])
            weight_sums.append(totals[number][-1])
        else:
            direction = grad * lax.rsqrt(prepared[number])
            counts.append(weight.shape[0] * group_size)
            weight_sums.append(totals[number][0])
        directions.append(direction)
        direction_sums.append(jnp.sum(direction * direction))
    direction_totals = [lax.psum(value_sum, "fsdp") for value_sum in direction_sums]
    new_params = []
    clips = []
    for number in range(12):
        weight = masters[number]
        clip_factor = jnp.maximum(
            1.0, jnp.sqrt(direction_totals[number] / counts[number]) / clip_level
        )
        rms_weight = jnp.sqrt(weight_sums[number] / counts[number])
        new_params.append(weight - step_rate * rms_weight * directions[number] / clip_factor)
        clips.append(clip_factor)
    clip_factors = jnp.stack(clips)
    new_rows_all = [prepared[2], prepared[4], prepared[8], prepared[10]]
    new_moments = [
        prepared[0],
        prepared[1],
        prepared[3],
        prepared[5],
        prepared[6],
        prepared[7],
        prepared[9],
        prepared[11],
    ]
    return (
        output,
        input_grad,
        grads[0],
        grads[1],
        grads[2],
        grads[3],
        grads[4],
        grads[5],
        grads[6],
        grads[7],
        grads[8],
        grads[9],
        grads[10],
        grads[11],
        new_rows_all[0],
        new_cols_all[0],
        new_rows_all[1],
        new_cols_all[1],
        new_rows_all[2],
        new_cols_all[2],
        new_rows_all[3],
        new_cols_all[3],
        new_moments[0],
        new_moments[1],
        new_moments[2],
        new_moments[3],
        new_moments[4],
        new_moments[5],
        new_moments[6],
        new_moments[7],
        new_params[0],
        new_params[1],
        new_params[2],
        new_params[3],
        new_params[4],
        new_params[5],
        new_params[6],
        new_params[7],
        new_params[8],
        new_params[9],
        new_params[10],
        new_params[11],
        clip_factors,
    )


def solution(mesh):
    in_specs = (
        P(("fsdp", "dp"), None),
        P(("fsdp", "dp"), None),
        P("fsdp"),
        P("fsdp"),
        P("fsdp", None),
        P("fsdp"),
        P("fsdp", None),
        P("fsdp"),
        P("fsdp"),
        P("fsdp"),
        P("fsdp", None),
        P("fsdp"),
        P("fsdp", None),
        P("fsdp"),
        P("fsdp"),
        P(),
        P("fsdp"),
        P(),
        P("fsdp"),
        P(),
        P("fsdp"),
        P(),
        P("fsdp"),
        P("fsdp"),
        P("fsdp"),
        P("fsdp"),
        P("fsdp"),
        P("fsdp"),
        P("fsdp"),
        P("fsdp"),
    )
    out_specs = (
        P(("fsdp", "dp"), None),
        P(("fsdp", "dp"), None),
        P("fsdp"),
        P("fsdp"),
        P("fsdp", None),
        P("fsdp"),
        P("fsdp", None),
        P("fsdp"),
        P("fsdp"),
        P("fsdp"),
        P("fsdp", None),
        P("fsdp"),
        P("fsdp", None),
        P("fsdp"),
        P("fsdp"),
        P(),
        P("fsdp"),
        P(),
        P("fsdp"),
        P(),
        P("fsdp"),
        P(),
        P("fsdp"),
        P("fsdp"),
        P("fsdp"),
        P("fsdp"),
        P("fsdp"),
        P("fsdp"),
        P("fsdp"),
        P("fsdp"),
        P("fsdp"),
        P("fsdp"),
        P("fsdp", None),
        P("fsdp"),
        P("fsdp", None),
        P("fsdp"),
        P("fsdp"),
        P("fsdp"),
        P("fsdp", None),
        P("fsdp"),
        P("fsdp", None),
        P("fsdp"),
        P(),
    )
    return jax.shard_map(
        on_device, mesh=mesh, in_specs=in_specs, out_specs=out_specs, check_vma=False
    )
```

profile of v0, /device:TPU:0, one launch (start us, length us, event | category | flops | bytes accessed | tf_op | source)
XLA Modules:
  0.0 1457.1 jit_solution(12676742999869469270)
XLA Ops:
  7.3 3.8 multiply_reduce_fusion.14
  14.8 4.3 multiply_reduce_fusion.7
  21.2 22.4 %all-gather.5 = bf16[8,1,128]{2,1,0:T(2,128)(2,1)S(1)} all-gather(bf16[1,1,128]{2,1,0:T(2,128)(2,1)S(1)} %get-tuple-element.209), channel_id=1, replica_groups=mesh['fsdp'=8,'dp'=4] {'fsdp'}, dimensions={0}, use_global_device_ids=true | all-gather | bytes 2304 | tf_op jit(solution)/shard_map/all_gather | solution.py:161
  44.2 16.4 %all-gather.4 = bf16[8,1,128]{2,1,0:T(2,128)(2,1)S(1)} all-gather(bf16[1,1,128]{2,1,0:T(2,128)(2,1)S(1)} %get-tuple-element.211), channel_id=1, replica_groups=mesh['fsdp'=8,'dp'=4] {'fsdp'}, dimensions={0}, use_global_device_ids=true | all-gather | bytes 2304 | tf_op jit(solution)/shard_map/all_gather | solution.py:160
  61.2 18.2 %all-gather.3 = bf16[8,1,128]{2,1,0:T(2,128)(2,1)S(1)} all-gather(bf16[1,1,128]{2,1,0:T(2,128)(2,1)S(1)} %get-tuple-element.213), channel_id=1, replica_groups=mesh['fsdp'=8,'dp'=4] {'fsdp'}, dimensions={0}, use_global_device_ids=true | all-gather | bytes 2304 | tf_op jit(solution)/shard_map/all_gather | solution.py:159
  80.0 16.5 %all-gather.1 = bf16[8,1,128]{2,1,0:T(2,128)(2,1)S(1)} all-gather(bf16[1,1,128]{2,1,0:T(2,128)(2,1)S(1)} %get-tuple-element.215), channel_id=1, replica_groups=mesh['fsdp'=8,'dp'=4] {'fsdp'}, dimensions={0}, use_global_device_ids=true | all-gather | bytes 2304 | tf_op jit(solution)/shard_map/all_gather | solution.py:155
  97.2 18.0 %all-gather = bf16[8,1,128]{2,1,0:T(2,128)(2,1)S(1)} all-gather(bf16[1,1,128]{2,1,0:T(2,128)(2,1)S(1)} %get-tuple-element.217), channel_id=1, replica_groups=mesh['fsdp'=8,'dp'=4] {'fsdp'}, dimensions={0}, use_global_device_ids=true | all-gather | bytes 2304 | tf_op jit(solution)/shard_map/all_gather | solution.py:154
  115.2 26.1 %all-gather.6 = bf16[8,1,512]{2,1,0:T(2,128)(2,1)S(1)} all-gather(bf16[1,1,512]{2,1,0:T(2,128)(2,1)S(1)} %reshape.379), channel_id=1, replica_groups=mesh['fsdp'=8,'dp'=4] {'fsdp'}, dimensions={0}, use_global_device_ids=true | all-gather | bytes 9216 | tf_op jit(solution)/shard_map/all_gather | solution.py:163
  141.3 17.0 %all-gather.2 = bf16[8,1,256]{2,1,0:T(2,128)(2,1)S(1)} all-gather(bf16[1,1,256]{2,1,0:T(2,128)(2,1)S(1)} %reshape.371), channel_id=1, replica_groups=mesh['fsdp'=8,'dp'=4] {'fsdp'}, dimensions={0}, use_global_device_ids=true | all-gather | bytes 4608 | tf_op jit(solution)/shard_map/all_gather | solution.py:157
  159.1 6.6 fusion.80
  171.5 2.9 copy.93
  174.5 10.1 multiply_reduce_fusion.1
  184.6 10.6 fusion.2
  195.1 11.5 fusion.60
  206.6 3.9 fusion.100
  211.6 78.3 %all-gather.21.cloned.1.call-done = bf16[1024,4096]{1,0:T(8,128)(2,1)} async-done(((bf16[128,4096]{1,0:T(8,128)(2,1)}), bf16[1024,4096]{1,0:T(8,128)(2,1)}) %all-gather.21.cloned.1.call-update) | async-done | bytes 8388624 | tf_op jit(solution)/shard_map/all_gather | solution.py:162
  289.9 11.4 fusion.85
  301.3 114.3 %all-gather.23.cloned.1.call-done = bf16[4096,1024]{1,0:T(8,128)(2,1)} async-done(((bf16[512,1024]{1,0:T(8,128)(2,1)}), bf16[4096,1024]{1,0:T(8,128)(2,1)}) %all-gather.23.cloned.1.call-update) | async-done | bytes 8388624 | tf_op jit(solution)/shard_map/all_gather | solution.py:164
  415.6 30.8 %convert_reduce_fusion = (f32[4096]{0:T(1024)S(1)}, bf16[577,4096]{1,0:T(8,128)(2,1)S(1)}, f32[577,4096]{1,0:T(8,128)}) fusion(f32[577,4096]{1,0:T(8,128)} %fusion.85, f32[4096]{0:T(1024)S(1)} %bitcast.135, bf16[577,1024]{1,0:T(8,128)(2,1)} %param.31, bf16[4096,1024]{1,0:T(8,128)(2,1)} %all-gather.23.cloned.1.call-done), kind=kOutput, calls=%fused_computation.22 | convolution fusion | flops 5017477120 | bytes 33236992 | tf_op jit(solution)/shard_map/dot_general | solution.py:39
  446.4 5.6 multiply_reduce_fusion.2
  460.4 13.6 fusion.101
  474.0 13.4 fusion.57
  487.5 32.9 %fusion.47 = bf16[16,64,577]{2,1,0:T(8,128)(2,1)} fusion(bf16[577,16,64]{0,2,1:T(8,128)(2,1)} %bitcast.120, f32[16,577,577]{1,2,0:T(8,128)} %fusion.101, f32[16,577,577]{1,2,0:T(8,128)} %get-tuple-element.219, f32[16,577]{1,0:T(8,128)S(1)} %copy-done.23), kind=kOutput, calls=%fused_computation.85 | convolution fusion | flops 746361600 | bytes 45015232 | tf_op jit(solution)/shard_map/while/body/eval_jaxpr/hqk,khd->qhd/dot_general | solution.py:93
  520.4 33.3 %fusion.52 = bf16[16,64,577]{2,1,0:T(8,128)(2,1)} fusion(bf16[577,16,64]{0,2,1:T(8,128)(2,1)} %bitcast.118, f32[16,577,577]{1,2,0:T(8,128)} %fusion.101, f32[16,577,577]{1,2,0:T(8,128)} %get-tuple-element.219, f32[16,577]{1,0:T(8,128)S(1)} %copy-done.23), kind=kOutput, calls=%fused_computation.86 | convolution fusion | flops 746361600 | bytes 45015232 | tf_op jit(solution)/shard_map/while/body/eval_jaxpr/hqk,qhd->khd/dot_general | solution.py:94
  553.7 12.5 fusion.78
  566.8 13.0 fusion.84
  580.1 12.0 multiply_convert_fusion.1
  592.0 12.5 fusion.103
  604.6 5.6 fusion.102
  610.3 109.6 %reduce-scatter.5.cloned.1.call-done = f32[32,3072]{1,0:T(8,128)} async-done(((f32[1024,3072]{1,0:T(8,128)}), f32[32,3072]{1,0:T(8,128)}) %reduce-scatter.5.cloned.1.call-update) | async-done | bytes 393232 | tf_op jit(solution)/shard_map/reduce_scatter | solution.py:251
  725.3 179.0 %reduce-scatter.9.cloned.1.call-done = f32[32,4096]{1,0:T(8,128)} async-done(((f32[1024,4096]{1,0:T(8,128)}), f32[32,4096]{1,0:T(8,128)}) %reduce-scatter.9.cloned.1.call-update) | async-done | bytes 524304 | tf_op jit(solution)/shard_map/reduce_scatter | solution.py:257
  904.6 8.8 fusion.86
  918.0 48.0 %all-reduce.15 = (f32[1024]{0:T(1024)S(1)}, f32[1024]{0:T(1024)S(1)}, f32[2048]{0:T(1024)S(1)}, f32[1024]{0:T(1024)S(1)}, f32[1024]{0:T(1024)S(1)}, /*index=5*/f...) all-reduce(f32[1024]{0:T(1024)S(1)} %get-tuple-element.84, ...), channel_id=2, replica_groups=mesh['fsdp'=8,'dp'=4] {'fsdp','dp'}, use_global_device_ids=true, to_apply=%region_12.13.clone | all-reduce | flops 12288 | bytes 98304
  967.1 125.8 %reduce-scatter.11.cloned.1.call-done = f32[128,1024]{1,0:T(8,128)} async-done(((f32[4096,1024]{1,0:T(8,128)}), f32[128,1024]{1,0:T(8,128)}) %reduce-scatter.11.cloned.1.call-update) | async-done | bytes 524304 | tf_op jit(solution)/shard_map/reduce_scatter | solution.py:259
  1093.1 6.0 all-reduce.18
  1099.1 5.0 all-gather.8
  1107.9 130.0 %reduce-scatter.7.cloned.1.call-done = f32[32,1024]{1,0:T(8,128)} async-done(((f32[1024,1024]{1,0:T(8,128)}), f32[32,1024]{1,0:T(8,128)}) %reduce-scatter.7.cloned.1.call-update) | async-done | bytes 131088 | tf_op jit(solution)/shard_map/reduce_scatter | solution.py:253
  1237.9 6.7 all_gather.88
  1246.8 8.3 all-gather.25.cloned.1.call-done
  1259.8 19.3 %all-gather.27.cloned.1.call-done = f32[128,4096]{1,0:T(8,128)} async-done(((f32[32,4096]{1,0:T(8,128)}), f32[128,4096]{1,0:T(8,128)}) %all-gather.27.cloned.1.call-update) | async-done | bytes 2097168 | tf_op jit(solution)/shard_map/all_gather | solution.py:271
  1279.2 3.2 multiply_reduce_fusion.11
  1283.0 20.4 %all-gather.29.cloned.1.call-done = f32[512,1024]{1,0:T(8,128)} async-done(((f32[128,1024]{1,0:T(8,128)}), f32[512,1024]{1,0:T(8,128)}) %all-gather.29.cloned.1.call-update) | async-done | bytes 2097168 | tf_op jit(solution)/shard_map/all_gather | solution.py:273
  1303.4 3.3 multiply_reduce_fusion.9
  1309.9 37.9 %all-reduce.17 = (f32[3074]{0:T(1024)S(1)}, f32[1026]{0:T(1024)S(1)}, f32[4098]{0:T(1024)S(1)}, f32[1026]{0:T(1024)S(1)}) all-reduce(f32[3074]{0:T(1024)S(1)} %concatenate.22, f32[1026]{0:T(1024)S(1)} %concatenate.23, f32[4098]{0:T(1024)S(1)} %concatenate.24, f32[1026]{0:T(1024)S(1)} %concatenate.25), channel_id=1, replica_groups=mesh['fsdp'=8,'dp'=4] {'fsdp'}, use_global_device_ids=true, to_apply=%region_35.36 | all-reduce | flops 9224 | bytes 73792 | tf_op jit(solution)/shard_map/psum | solution.py:314
  1362.4 33.0 %all-reduce.16 = (f32[]{:T(128)}, f32[1]{0:T(128)}, f32[]{:T(128)}, f32[1]{0:T(128)}, f32[]{:T(128)}, /*index=5*/f32[]{:T(128)}, f32[1]{0:T(128)}, f32[]{:T(128)...) all-reduce(f32[]{:T(128)} %get-tuple-element.230, ...), channel_id=1, replica_groups=mesh['fsdp'=8,'dp'=4] {'fsdp'}, use_global_device_ids=true, to_apply=%region_54.55 | all-reduce | flops 20 | bytes 160 | tf_op jit(solution)/shard_map/psum | solution.py:339
  1410.5 16.5 %all-gather.7 = bf16[8,1,128]{2,1,0:T(2,128)(2,1)S(1)} all-gather(bf16[1,1,128]{2,1,0:T(2,128)(2,1)S(1)} %get-tuple-element.207), channel_id=1, replica_groups=mesh['fsdp'=8,'dp'=4] {'fsdp'}, dimensions={0}, use_global_device_ids=true | all-gather | bytes 2304 | tf_op jit(solution)/shard_map/all_gather | solution.py:165
  1428.0 3.1 divide_subtract_fusion.2
  1440.5 9.7 add_convert_fusion.2
  (306 shorter events, 70.3 us)
Async XLA Ops:
  7.3 151.8 %all-gather.17.cloned.1.call-start = ((), (), s32[]{:S(2)}) async-start(), calls=%async_computation.4 | async-start | bytes 7077888 | tf_op jit(solution)/shard_map/all_gather | solution.py:156
  11.2 195.5 %all-gather.19.cloned.1.call-start = ((), (), s32[]{:S(2)}) async-start(), calls=%async_computation.5 | async-start | bytes 2359296 | tf_op jit(solution)/shard_map/all_gather | solution.py:158
  12.6 277.3 %all-gather.21.cloned.1.call-start = ((), (), s32[]{:S(2)}) async-start(), calls=%async_computation.6 | async-start | bytes 9437184 | tf_op jit(solution)/shard_map/all_gather | solution.py:162
  14.8 81.8 %copy-start.79 = (f32[128]{0:T(128)S(1)}, f32[128]{0:T(128)}, u32[]{:S(2)}) copy-start(f32[128]{0:T(128)} %param.32) | copy-start | bytes 1540
  14.8 143.5 %copy-start.2 = (bf16[577,1024]{1,0:T(8,128)(2,1)S(1)}, bf16[577,1024]{1,0:T(8,128)(2,1)}, u32[]{:S(2)}) copy-start(bf16[577,1024]{1,0:T(8,128)(2,1)} %param.30) | copy-start | bytes 3545092
  14.8 400.8 %all-gather.23.cloned.1.call-start = ((), (), s32[]{:S(2)}) async-start(), calls=%async_computation.7 | async-start | bytes 9437184 | tf_op jit(solution)/shard_map/all_gather | solution.py:164
  19.2 700.7 %reduce-scatter.5.cloned.1.call-start = ((), (), s32[]{:S(2)}) async-start(), calls=%async_computation.8 | async-start | bytes 12976128 | tf_op jit(solution)/shard_map/reduce_scatter | solution.py:251
  43.6 246.3 %copy-start.21 = (f32[8,1,128]{2,1,0:T(1,128)}, f32[8,1,128]{2,1,0:T(1,128)S(1)}, u32[]{:S(2)}) copy-start(f32[8,1,128]{2,1,0:T(1,128)S(1)} %convert_element_type.176) | copy-start | bytes 12292
  566.2 338.1 %reduce-scatter.9.cloned.1.call-start = ((), (), s32[]{:S(2)}) async-start(), calls=%async_computation.11 | async-start | bytes 17301504 | tf_op jit(solution)/shard_map/reduce_scatter | solution.py:257
  579.8 513.0 %reduce-scatter.11.cloned.1.call-start = ((), (), s32[]{:S(2)}) async-start(), calls=%async_computation.13 | async-start | bytes 17301504 | tf_op jit(solution)/shard_map/reduce_scatter | solution.py:259
  604.6 633.3 %reduce-scatter.7.cloned.1.call-start = ((), (), s32[]{:S(2)}) async-start(), calls=%async_computation.10 | async-start | bytes 4325376 | tf_op jit(solution)/shard_map/reduce_scatter | solution.py:253
  610.2 109.8 %copy-start.91 = (u32[32]{0:T(128)S(1)}, u32[32]{0:T(128)}, u32[]{:S(2)}) copy-start(u32[32]{0:T(128)} %constant.266) | copy-start | bytes 388
  610.2 111.6 %copy-start.75 = (f32[128]{0:T(128)S(1)}, f32[128]{0:T(128)}, u32[]{:S(2)}) copy-start(f32[128]{0:T(128)} %param.43) | copy-start | bytes 1540
  610.2 644.8 %all-gather.25.cloned.1.call-start = ((), (), s32[]{:S(2)}) async-start(), calls=%async_computation.9 | async-start | bytes 1966080 | tf_op jit(solution)/shard_map/all_gather | solution.py:265
  719.9 559.3 %all-gather.27.cloned.1.call-start = ((), (), s32[]{:S(2)}) async-start(), calls=%async_computation.12 | async-start | bytes 2621440 | tf_op jit(solution)/shard_map/all_gather | solution.py:271
  904.3 399.1 %all-gather.29.cloned.1.call-start = ((), (), s32[]{:S(2)}) async-start(), calls=%async_computation.14 | async-start | bytes 2621440 | tf_op jit(solution)/shard_map/all_gather | solution.py:273
  915.7 188.4 %copy-start.68 = (f32[256]{0:T(256)S(1)}, f32[256]{0:T(256)}, u32[]{:S(2)}) copy-start(f32[256]{0:T(256)} %param.54) | copy-start | bytes 3076
  915.7 189.0 %copy-start.69 = (f32[128]{0:T(128)S(1)}, f32[128]{0:T(128)}, u32[]{:S(2)}) copy-start(f32[128]{0:T(128)} %param.53) | copy-start | bytes 1540
  915.7 189.0 %copy-start.70 = (f32[128]{0:T(128)S(1)}, f32[128]{0:T(128)}, u32[]{:S(2)}) copy-start(f32[128]{0:T(128)} %param.52) | copy-start | bytes 1540
  915.7 189.6 %copy-start.71 = (f32[128]{0:T(128)S(1)}, f32[128]{0:T(128)}, u32[]{:S(2)}) copy-start(f32[128]{0:T(128)} %param.56) | copy-start | bytes 1540
  915.8 189.6 %copy-start.72 = (f32[128]{0:T(128)S(1)}, f32[128]{0:T(128)}, u32[]{:S(2)}) copy-start(f32[128]{0:T(128)} %param.55) | copy-start | bytes 1540
  915.8 190.3 %copy-start.73 = (f32[128]{0:T(128)S(1)}, f32[128]{0:T(128)}, u32[]{:S(2)}) copy-start(f32[128]{0:T(128)} %param.59) | copy-start | bytes 1540
  915.8 190.3 %copy-start.74 = (f32[128]{0:T(128)S(1)}, f32[128]{0:T(128)}, u32[]{:S(2)}) copy-start(f32[128]{0:T(128)} %param.57) | copy-start | bytes 1540
  915.8 191.5 %copy-start.56 = (f32[512]{0:T(512)S(1)}, f32[512]{0:T(512)}, u32[]{:S(2)}) copy-start(f32[512]{0:T(512)} %param.58) | copy-start | bytes 6148
  918.0 326.7 %copy-start.76 = (f32[128]{0:T(128)S(1)}, f32[128]{0:T(128)}, u32[]{:S(2)}) copy-start(f32[128]{0:T(128)} %param.46) | copy-start | bytes 1540
  1104.1 332.0 %copy-start.37 = (f32[4,1,128]{2,1,0:T(1,128)}, f32[4,1,128]{2,1,0:T(1,128)S(1)}, u32[]{:S(2)}) copy-start(f32[4,1,128]{2,1,0:T(1,128)S(1)} %broadcast_multiply_fusion.6) | copy-start | bytes 6148
  1104.7 334.6 %copy-start.50 = (f32[256]{0:T(256)}, f32[256]{0:T(256)S(1)}, u32[]{:S(2)}) copy-start(f32[256]{0:T(256)S(1)} %get-tuple-element.151) | copy-start | bytes 3076
  1104.7 334.6 %copy-start.51 = (f32[256]{0:T(256)}, f32[256]{0:T(256)S(1)}, u32[]{:S(2)}) copy-start(f32[256]{0:T(256)S(1)} %get-tuple-element.152) | copy-start | bytes 3076
  1105.4 331.3 %copy-start.60 = (f32[128]{0:T(128)}, f32[128]{0:T(128)S(1)}, u32[]{:S(2)}) copy-start(f32[128]{0:T(128)S(1)} %get-tuple-element.231) | copy-start | bytes 1540
  1105.4 331.3 %copy-start.61 = (f32[128]{0:T(128)}, f32[128]{0:T(128)S(1)}, u32[]{:S(2)}) copy-start(f32[128]{0:T(128)S(1)} %get-tuple-element.232) | copy-start | bytes 1540
  1105.4 331.8 %copy-start.58 = (f32[128]{0:T(128)}, f32[128]{0:T(128)S(1)}, u32[]{:S(2)}) copy-start(f32[128]{0:T(128)S(1)} %get-tuple-element.154) | copy-start | bytes 1540
  1105.4 331.9 %copy-start.59 = (f32[128]{0:T(128)}, f32[128]{0:T(128)S(1)}, u32[]{:S(2)}) copy-start(f32[128]{0:T(128)S(1)} %get-tuple-element.155) | copy-start | bytes 1540
  1106.0 331.7 %copy-start.64 = (f32[128]{0:T(128)}, f32[128]{0:T(128)S(1)}, u32[]{:S(2)}) copy-start(f32[128]{0:T(128)S(1)} %get-tuple-element.228) | copy-start | bytes 1540
  1106.0 331.7 %copy-start.65 = (f32[128]{0:T(128)}, f32[128]{0:T(128)S(1)}, u32[]{:S(2)}) copy-start(f32[128]{0:T(128)S(1)} %get-tuple-element.229) | copy-start | bytes 1540
  1106.0 332.2 %copy-start.62 = (f32[128]{0:T(128)}, f32[128]{0:T(128)S(1)}, u32[]{:S(2)}) copy-start(f32[128]{0:T(128)S(1)} %get-tuple-element.145) | copy-start | bytes 1540
  1106.0 332.3 %copy-start.63 = (f32[128]{0:T(128)}, f32[128]{0:T(128)S(1)}, u32[]{:S(2)}) copy-start(f32[128]{0:T(128)S(1)} %get-tuple-element.146) | copy-start | bytes 1540
  1107.2 301.9 %copy-start.54 = (f32[128]{0:T(128)}, f32[128]{0:T(128)S(1)}, u32[]{:S(2)}) copy-start(f32[128]{0:T(128)S(1)} %get-tuple-element.137) | copy-start | bytes 1540
  1107.2 301.9 %copy-start.55 = (f32[128]{0:T(128)}, f32[128]{0:T(128)S(1)}, u32[]{:S(2)}) copy-start(f32[128]{0:T(128)S(1)} %get-tuple-element.138) | copy-start | bytes 1540
  1107.9 328.2 %copy-start.42 = (f32[512]{0:T(512)}, f32[512]{0:T(512)S(1)}, u32[]{:S(2)}) copy-start(f32[512]{0:T(512)S(1)} %get-tuple-element.140) | copy-start | bytes 6148
  1107.9 150.0 %copy-start.77 = (f32[128]{0:T(128)S(1)}, f32[128]{0:T(128)}, u32[]{:S(2)}) copy-start(f32[128]{0:T(128)} %param.44) | copy-start | bytes 1540
  1244.7 182.2 %copy-start.17 = (f32[128,1024]{1,0:T(8,128)}, f32[128,1024]{1,0:T(8,128)S(1)}, u32[]{:S(2)}) copy-start(f32[128,1024]{1,0:T(8,128)S(1)} %get-tuple-element.167) | copy-start | bytes 1572868
  1245.4 181.6 %copy-start.44 = (f32[128]{0:T(128)}, f32[128]{0:T(128)S(1)}, u32[]{:S(2)}) copy-start(f32[128]{0:T(128)S(1)} %get-tuple-element.166) | copy-start | bytes 1540
  1258.5 169.5 %copy-start.43 = (f32[128]{0:T(128)}, f32[128]{0:T(128)S(1)}, u32[]{:S(2)}) copy-start(f32[128]{0:T(128)S(1)} %get-tuple-element.169) | copy-start | bytes 1540
  1283.0 148.1 %copy-start.45 = (f32[128]{0:T(128)}, f32[128]{0:T(128)S(1)}, u32[]{:S(2)}) copy-start(f32[128]{0:T(128)S(1)} %get-tuple-element.163) | copy-start | bytes 1540
  1307.3 125.8 %copy-start.36 = (f32[512]{0:T(512)}, f32[512]{0:T(512)S(1)}, u32[]{:S(2)}) copy-start(f32[512]{0:T(512)S(1)} %get-tuple-element.160) | copy-start | bytes 6148
  1351.2 76.8 %copy-start.25 = (f32[3072]{0:T(1024)}, f32[3072]{0:T(1024)S(1)}, u32[]{:S(2)}) copy-start(f32[3072]{0:T(1024)S(1)} %fusion.63) | copy-start | bytes 36868
  1351.2 79.9 %copy-start.24 = (f32[4096]{0:T(1024)}, f32[4096]{0:T(1024)S(1)}, u32[]{:S(2)}) copy-start(f32[4096]{0:T(1024)S(1)} %fusion.62) | copy-start | bytes 49156
  1354.5 78.5 %copy-start.35 = (f32[1024]{0:T(1024)}, f32[1024]{0:T(1024)S(1)}, u32[]{:S(2)}) copy-start(f32[1024]{0:T(1024)S(1)} %get-tuple-element.233) | copy-start | bytes 12292
  (55 other events, 1095.6 us)
Sparse Core Ops, SparseCore 0:
  11.3 101.9 all-gather.16
  116.0 47.6 all-gather.18
  166.4 123.4 all-gather.20
  292.4 123.1 all-gather.22
  566.3 153.5 reduce-scatter.4
  722.1 182.1 reduce-scatter.8
  906.7 186.1 reduce-scatter.10
  1095.2 142.5 reduce-scatter.6
  1239.5 15.5 all-gather.24
  1256.5 22.5 all-gather.26
  1280.8 22.5 all-gather.28
where the time goes:
time: 1460 us
  waiting for transfers between devices  785 us (54%)
  blocking collectives  288 us (20%)
  matrix products  238 us (16%)
  other arithmetic  86.3 us (6%)
  between operations  35.5 us (2%)
  local copies, waits for them, and re-layouts  23.8 us (2%)
    reduce_scatter x1, waiting for transfers between devices, on_device(): lax.psum_scatter(terms[8], ('fsdp', 'dp'), scatter_dimension=0, tiled=True)  179 us
    reduce_scatter x1, waiting for transfers between devices, on_device(): lax.psum_scatter(terms[4], ('fsdp', 'dp'), scatter_dimension=0, tiled=True)  130 us
    reduce_scatter x1, waiting for transfers between devices, on_device(): lax.psum_scatter(terms[10], ('fsdp', 'dp'), scatter_dimension=0, tiled=True)  126 us
    all_gather x1, waiting for transfers between devices, on_device(): lax.all_gather(halves[10], 'fsdp', axis=0, tiled=True)  114 us
    reduce_scatter x1, waiting for transfers between devices, on_device(): lax.psum_scatter(terms[2], ('fsdp', 'dp'), scatter_dimension=0, tiled=True)  110 us
    all_gather x1, waiting for transfers between devices, on_device(): lax.all_gather(halves[8], 'fsdp', axis=0, tiled=True)  78.3 us
    unnamed x2, blocking collectives  54.1 us
    dot_general x4, matrix products, tail_dot(): lax.dot_general(left, right, (((1,), (1,)), ((), ())), preferred_element_...  47.7 us
  transfers between devices with their start and end apart: 11, of which 9 were waited for; matrix products, arithmetic and copies ran while one was open for 10% of the time, Pallas kernels for 0%

commit v1 on v0

--- a/solution.py
+++ b/solution.py
@@ -3,6 +3,7 @@
 import jax.numpy as jnp
 from jax import lax
 from jax.sharding import PartitionSpec as P
+from jax.lax import all_gather
 
 HEAD_DIM = 64
 SEQ = 577
@@ -135,6 +136,11 @@
     in_bias_moment,
     down_bias_moment,
 ):
+
+    def _serve_sample(mat, across="fsdp"):
+        low = all_gather(mat, across)
+        return jnp.sum(low, axis=0)
+
     masters = [
         norm1_gain,
         norm1_bias,
@@ -311,7 +317,7 @@
             position = vector_slots[number]
             prepared.append(0.5 * moments[position] + 0.5 * squared)
             packs.append(jnp.sum(weight * weight).reshape(1))
-    totals = [lax.psum(packed, "fsdp") for packed in packs]
+    totals = [_serve_sample(packed) for packed in packs]
     directions = []
     counts = []
     weight_sums = []

time: 1460 us -> 1580 us (1.082)
  waiting for transfers between devices: 785 us -> 895 us
  blocking collectives: 288 us -> 251 us
  local copies, waits for them, and re-layouts: 23.8 us -> 46 us
    unnamed x11 -> x15, waiting for transfers between devices: 0.18 us -> 133 us
    reduce_scatter x1, waiting for transfers between devices: 179 us -> 126 us  [on_device(): lax.psum_scatter(terms[8], ('fsdp', 'dp'), scatter_dimension=0, tiled=True)]
    reduce_scatter x1, waiting for transfers between devices: 126 us -> 165 us  [on_device(): lax.psum_scatter(terms[10], ('fsdp', 'dp'), scatter_dimension=0, tiled=True)]
    psum x1 -> x0, blocking collectives: 37.9 us -> none  [on_device(): totals = [lax.psum(packed, 'fsdp') for packed in packs]]
  transfers between devices with their start and end apart: 11 -> 13, of which waited for: 9 -> 11; matrix products, arithmetic and copies ran while one was open for 10% -> 12% of each run, Pallas kernels for 0% -> 0%
where the time goes in v1:
time: 1580 us; the launch traced here: 1570 us
  waiting for transfers between devices  895 us (57%)
  blocking collectives  251 us (16%)
  matrix products  242 us (15%)
  other arithmetic  99.3 us (6%)
  local copies, waits for them, and re-layouts  46 us (3%)
  between operations  37.7 us (2%)
    reduce_scatter x1, waiting for transfers between devices, on_device(): lax.psum_scatter(terms[10], ('fsdp', 'dp'), scatter_dimension=0, tiled=True)  165 us
    unnamed x15, waiting for transfers between devices  133 us
    reduce_scatter x1, waiting for transfers between devices, on_device(): lax.psum_scatter(terms[4], ('fsdp', 'dp'), scatter_dimension=0, tiled=True)  129 us
    reduce_scatter x1, waiting for transfers between devices, on_device(): lax.psum_scatter(terms[8], ('fsdp', 'dp'), scatter_dimension=0, tiled=True)  126 us
    all_gather x1, waiting for transfers between devices, on_device(): lax.all_gather(halves[10], 'fsdp', axis=0, tiled=True)  114 us
    reduce_scatter x1, waiting for transfers between devices, on_device(): lax.psum_scatter(terms[2], ('fsdp', 'dp'), scatter_dimension=0, tiled=True)  110 us
    all_gather x1, waiting for transfers between devices, on_device(): lax.all_gather(halves[8], 'fsdp', axis=0, tiled=True)  73.8 us
    unnamed x2, blocking collectives  53.8 us
  transfers between devices with their start and end apart: 13, of which 11 were waited for; matrix products, arithmetic and copies ran while one was open for 12% of the time, Pallas kernels for 0%

profile of v1, /device:TPU:0, one launch (start us, length us, event | category | flops | bytes accessed | tf_op | source)
XLA Modules:
  0.0 1572.1 jit_solution(8302127363680468905)
XLA Ops:
  7.3 3.8 multiply_reduce_fusion.14
  14.8 4.4 multiply_reduce_fusion.7
  21.1 22.4 %all-gather.9 = bf16[8,1,128]{2,1,0:T(2,128)(2,1)S(1)} all-gather(bf16[1,1,128]{2,1,0:T(2,128)(2,1)S(1)} %get-tuple-element.209), channel_id=1, replica_groups=mesh['fsdp'=8,'dp'=4] {'fsdp'}, dimensions={0}, use_global_device_ids=true | all-gather | bytes 2304 | tf_op jit(solution)/shard_map/all_gather | solution.py:167
  44.2 16.4 %all-gather.8 = bf16[8,1,128]{2,1,0:T(2,128)(2,1)S(1)} all-gather(bf16[1,1,128]{2,1,0:T(2,128)(2,1)S(1)} %get-tuple-element.211), channel_id=1, replica_groups=mesh['fsdp'=8,'dp'=4] {'fsdp'}, dimensions={0}, use_global_device_ids=true | all-gather | bytes 2304 | tf_op jit(solution)/shard_map/all_gather | solution.py:166
  61.1 18.2 %all-gather.7 = bf16[8,1,128]{2,1,0:T(2,128)(2,1)S(1)} all-gather(bf16[1,1,128]{2,1,0:T(2,128)(2,1)S(1)} %get-tuple-element.213), channel_id=1, replica_groups=mesh['fsdp'=8,'dp'=4] {'fsdp'}, dimensions={0}, use_global_device_ids=true | all-gather | bytes 2304 | tf_op jit(solution)/shard_map/all_gather | solution.py:165
  80.0 16.5 %all-gather.5 = bf16[8,1,128]{2,1,0:T(2,128)(2,1)S(1)} all-gather(bf16[1,1,128]{2,1,0:T(2,128)(2,1)S(1)} %get-tuple-element.215), channel_id=1, replica_groups=mesh['fsdp'=8,'dp'=4] {'fsdp'}, dimensions={0}, use_global_device_ids=true | all-gather | bytes 2304 | tf_op jit(solution)/shard_map/all_gather | solution.py:161
  97.1 18.0 %all-gather.4 = bf16[8,1,128]{2,1,0:T(2,128)(2,1)S(1)} all-gather(bf16[1,1,128]{2,1,0:T(2,128)(2,1)S(1)} %get-tuple-element.217), channel_id=1, replica_groups=mesh['fsdp'=8,'dp'=4] {'fsdp'}, dimensions={0}, use_global_device_ids=true | all-gather | bytes 2304 | tf_op jit(solution)/shard_map/all_gather | solution.py:160
  115.1 26.1 %all-gather.10 = bf16[8,1,512]{2,1,0:T(2,128)(2,1)S(1)} all-gather(bf16[1,1,512]{2,1,0:T(2,128)(2,1)S(1)} %reshape.363), channel_id=1, replica_groups=mesh['fsdp'=8,'dp'=4] {'fsdp'}, dimensions={0}, use_global_device_ids=true | all-gather | bytes 9216 | tf_op jit(solution)/shard_map/all_gather | solution.py:169
  141.2 16.4 %all-gather.6 = bf16[8,1,256]{2,1,0:T(2,128)(2,1)S(1)} all-gather(bf16[1,1,256]{2,1,0:T(2,128)(2,1)S(1)} %reshape.355), channel_id=1, replica_groups=mesh['fsdp'=8,'dp'=4] {'fsdp'}, dimensions={0}, use_global_device_ids=true | all-gather | bytes 4608 | tf_op jit(solution)/shard_map/all_gather | solution.py:163
  158.5 7.1 fusion.80
  176.0 13.3 multiply_reduce_fusion.1
  189.2 10.5 fusion.2
  199.8 11.4 fusion.60
  211.2 3.9 fusion.100
  216.1 73.8 %all-gather.25.cloned.1.call-done = bf16[1024,4096]{1,0:T(8,128)(2,1)} async-done(((bf16[128,4096]{1,0:T(8,128)(2,1)}), bf16[1024,4096]{1,0:T(8,128)(2,1)}) %all-gather.25.cloned.1.call-update) | async-done | bytes 8388624 | tf_op jit(solution)/shard_map/all_gather | solution.py:168
  289.9 11.4 fusion.85
  301.3 114.2 %all-gather.27.cloned.1.call-done = bf16[4096,1024]{1,0:T(8,128)(2,1)} async-done(((bf16[512,1024]{1,0:T(8,128)(2,1)}), bf16[4096,1024]{1,0:T(8,128)(2,1)}) %all-gather.27.cloned.1.call-update) | async-done | bytes 8388624 | tf_op jit(solution)/shard_map/all_gather | solution.py:170
  415.6 30.8 %convert_reduce_fusion = (f32[4096]{0:T(1024)S(1)}, bf16[577,4096]{1,0:T(8,128)(2,1)S(1)}, f32[577,4096]{1,0:T(8,128)}) fusion(f32[577,4096]{1,0:T(8,128)} %fusion.85, f32[4096]{0:T(1024)S(1)} %bitcast.131, bf16[577,1024]{1,0:T(8,128)(2,1)} %param.31, bf16[4096,1024]{1,0:T(8,128)(2,1)} %all-gather.27.cloned.1.call-done), kind=kOutput, calls=%fused_computation.22 | convolution fusion | flops 5017477120 | bytes 33236992 | tf_op jit(solution)/shard_map/dot_general | solution.py:40
  446.4 5.6 multiply_reduce_fusion.2
  460.5 13.6 fusion.101
  474.1 13.4 fusion.57
  487.5 32.9 %fusion.47 = bf16[16,64,577]{2,1,0:T(8,128)(2,1)} fusion(bf16[577,16,64]{0,2,1:T(8,128)(2,1)} %bitcast.116, f32[16,577,577]{1,2,0:T(8,128)} %fusion.101, f32[16,577,577]{1,2,0:T(8,128)} %get-tuple-element.219, f32[16,577]{1,0:T(8,128)S(1)} %copy-done.23), kind=kOutput, calls=%fused_computation.85 | convolution fusion | flops 746361600 | bytes 45015232 | tf_op jit(solution)/shard_map/while/body/eval_jaxpr/hqk,khd->qhd/dot_general | solution.py:94
  520.4 33.3 %fusion.52 = bf16[16,64,577]{2,1,0:T(8,128)(2,1)} fusion(bf16[577,16,64]{0,2,1:T(8,128)(2,1)} %bitcast.114, f32[16,577,577]{1,2,0:T(8,128)} %fusion.101, f32[16,577,577]{1,2,0:T(8,128)} %get-tuple-element.219, f32[16,577]{1,0:T(8,128)S(1)} %copy-done.23), kind=kOutput, calls=%fused_computation.86 | convolution fusion | flops 746361600 | bytes 45015232 | tf_op jit(solution)/shard_map/while/body/eval_jaxpr/hqk,qhd->khd/dot_general | solution.py:95
  553.7 12.5 fusion.78
  566.3 11.5 multiply_convert_fusion.1
  577.8 12.7 fusion.103
  591.2 13.3 fusion.84
  604.5 5.5 fusion.102
  610.1 109.8 %reduce-scatter.5.cloned.1.call-done = f32[32,3072]{1,0:T(8,128)} async-done(((f32[1024,3072]{1,0:T(8,128)}), f32[32,3072]{1,0:T(8,128)}) %reduce-scatter.5.cloned.1.call-update) | async-done | bytes 393232 | tf_op jit(solution)/shard_map/reduce_scatter | solution.py:257
  739.3 165.1 %reduce-scatter.11.cloned.1.call-done = f32[128,1024]{1,0:T(8,128)} async-done(((f32[4096,1024]{1,0:T(8,128)}), f32[128,1024]{1,0:T(8,128)}) %reduce-scatter.11.cloned.1.call-update) | async-done | bytes 524304 | tf_op jit(solution)/shard_map/reduce_scatter | solution.py:265
  904.7 8.8 fusion.86
  918.0 48.1 %all-reduce.27 = (f32[1024]{0:T(1024)S(1)}, f32[1024]{0:T(1024)S(1)}, f32[2048]{0:T(1024)S(1)}, f32[1024]{0:T(1024)S(1)}, f32[1024]{0:T(1024)S(1)}, /*index=5*/f...) all-reduce(f32[1024]{0:T(1024)S(1)} %get-tuple-element.84, ...), channel_id=6, replica_groups=mesh['fsdp'=8,'dp'=4] {'fsdp','dp'}, use_global_device_ids=true, to_apply=%region_12.13.clone | all-reduce | flops 12288 | bytes 98304
  967.2 126.2 %reduce-scatter.9.cloned.1.call-done = f32[32,4096]{1,0:T(8,128)} async-done(((f32[1024,4096]{1,0:T(8,128)}), f32[32,4096]{1,0:T(8,128)}) %reduce-scatter.9.cloned.1.call-update) | async-done | bytes 524304 | tf_op jit(solution)/shard_map/reduce_scatter | solution.py:263
  1093.6 5.7 all-reduce.31
  1099.4 5.0 all-gather.12
  1110.3 128.5 %reduce-scatter.7.cloned.1.call-done = f32[32,1024]{1,0:T(8,128)} async-done(((f32[1024,1024]{1,0:T(8,128)}), f32[32,1024]{1,0:T(8,128)}) %reduce-scatter.7.cloned.1.call-update) | async-done | bytes 131088 | tf_op jit(solution)/shard_map/reduce_scatter | solution.py:259
  1238.8 6.7 all_gather.136
  1248.0 8.0 all-gather.29.cloned.1.call-done
  1261.7 18.4 %all-gather.33.cloned.1.call-done = f32[512,1024]{1,0:T(8,128)} async-done(((f32[128,1024]{1,0:T(8,128)}), f32[512,1024]{1,0:T(8,128)}) %all-gather.33.cloned.1.call-update) | async-done | bytes 2097168 | tf_op jit(solution)/shard_map/all_gather | solution.py:279
  1280.1 3.3 multiply_reduce_fusion.9
  1286.6 17.8 %all-gather.31.cloned.1.call-done = f32[128,4096]{1,0:T(8,128)} async-done(((f32[32,4096]{1,0:T(8,128)}), f32[128,4096]{1,0:T(8,128)}) %all-gather.31.cloned.1.call-update) | async-done | bytes 2097168 | tf_op jit(solution)/shard_map/all_gather | solution.py:277
  1304.4 3.2 multiply_reduce_fusion.11
  1311.2 66.8 %all-reduce.35.cloned.1.call-done = (f32[8208]{0:T(1024)}, f32[8208]{0:T(1024)}) async-done(((f32[8208]{0:T(1024)}, f32[8208]{0:T(1024)}), (f32[8208]{0:T(1024)}, f32[8208]{0:T(1024)})) %all-reduce.35.cloned.1.call-update) | async-done | bytes 65680
  1387.5 66.1 %all-reduce.37.cloned.1.call-done = (f32[24592]{0:T(1024)}, f32[32784]{0:T(1024)}) async-done(((f32[24592]{0:T(1024)}, f32[32784]{0:T(1024)}), (f32[24592]{0:T(1024)}, f32[32784]{0:T(1024)})) %all-reduce.37.cloned.1.call-update) | async-done | bytes 229520
  1469.4 35.2 %all-reduce.28 = (f32[]{:T(128)}, f32[8]{0:T(128)S(1)}, f32[]{:T(128)}, f32[8]{0:T(128)S(1)}, f32[]{:T(128)}, /*index=5*/f32[]{:T(128)}, f32[8]{0:T(128)S(1)}, f...) all-reduce(f32[]{:T(128)} %get-tuple-element.230, ...), channel_id=1, replica_groups=mesh['fsdp'=8,'dp'=4] {'fsdp'}, use_global_device_ids=true, to_apply=%region_54.55 | all-reduce | flops 76 | bytes 608 | tf_op jit(solution)/shard_map/psum | solution.py:345
  1524.6 16.5 %all-gather.11 = bf16[8,1,128]{2,1,0:T(2,128)(2,1)S(1)} all-gather(bf16[1,1,128]{2,1,0:T(2,128)(2,1)S(1)} %get-tuple-element.207), channel_id=1, replica_groups=mesh['fsdp'=8,'dp'=4] {'fsdp'}, dimensions={0}, use_global_device_ids=true | all-gather | bytes 2304 | tf_op jit(solution)/shard_map/all_gather | solution.py:171
  1542.8 3.1 divide_subtract_fusion.2
  1555.5 9.7 add_convert_fusion.2
  (370 shorter events, 109.2 us)
Async XLA Ops:
  7.3 151.2 %all-gather.21.cloned.1.call-start = ((), (), s32[]{:S(2)}) async-start(), calls=%async_computation.4 | async-start | bytes 7077888 | tf_op jit(solution)/shard_map/all_gather | solution.py:162
  11.2 200.0 %all-gather.23.cloned.1.call-start = ((), (), s32[]{:S(2)}) async-start(), calls=%async_computation.5 | async-start | bytes 2359296 | tf_op jit(solution)/shard_map/all_gather | solution.py:164
  12.6 277.3 %all-gather.25.cloned.1.call-start = ((), (), s32[]{:S(2)}) async-start(), calls=%async_computation.6 | async-start | bytes 9437184 | tf_op jit(solution)/shard_map/all_gather | solution.py:168
  14.7 45.8 %copy-start.90 = (f32[128]{0:T(128)S(1)}, f32[128]{0:T(128)}, u32[]{:S(2)}) copy-start(f32[128]{0:T(128)} %param.37) | copy-start | bytes 1540
  14.8 64.6 %copy-start.94 = (f32[128]{0:T(128)S(1)}, f32[128]{0:T(128)}, u32[]{:S(2)}) copy-start(f32[128]{0:T(128)} %param.33) | copy-start | bytes 1540
  14.8 81.7 %copy-start.92 = (f32[128]{0:T(128)S(1)}, f32[128]{0:T(128)}, u32[]{:S(2)}) copy-start(f32[128]{0:T(128)} %param.32) | copy-start | bytes 1540
  14.8 142.9 %copy-start.2 = (bf16[577,1024]{1,0:T(8,128)(2,1)S(1)}, bf16[577,1024]{1,0:T(8,128)(2,1)}, u32[]{:S(2)}) copy-start(bf16[577,1024]{1,0:T(8,128)(2,1)} %param.30) | copy-start | bytes 3545092
  14.8 400.8 %all-gather.27.cloned.1.call-start = ((), (), s32[]{:S(2)}) async-start(), calls=%async_computation.7 | async-start | bytes 9437184 | tf_op jit(solution)/shard_map/all_gather | solution.py:170
  19.2 700.7 %reduce-scatter.5.cloned.1.call-start = ((), (), s32[]{:S(2)}) async-start(), calls=%async_computation.8 | async-start | bytes 12976128 | tf_op jit(solution)/shard_map/reduce_scatter | solution.py:257
  43.5 246.3 %copy-start.21 = (f32[8,1,128]{2,1,0:T(1,128)}, f32[8,1,128]{2,1,0:T(1,128)S(1)}, u32[]{:S(2)}) copy-start(f32[8,1,128]{2,1,0:T(1,128)S(1)} %convert_element_type.176) | copy-start | bytes 12292
  96.5 69.1 %copy-start.49 = (f32[8,1,128]{2,1,0:T(1,128)}, f32[8,1,128]{2,1,0:T(1,128)S(1)}, u32[]{:S(2)}) copy-start(f32[8,1,128]{2,1,0:T(1,128)S(1)} %convert_element_type.172) | copy-start | bytes 12292
  115.1 50.5 %copy-start.30 = (f32[8,1,128]{2,1,0:T(1,128)}, f32[8,1,128]{2,1,0:T(1,128)S(1)}, u32[]{:S(2)}) copy-start(f32[8,1,128]{2,1,0:T(1,128)S(1)} %convert_element_type.171) | copy-start | bytes 12292
  566.3 338.1 %reduce-scatter.11.cloned.1.call-start = ((), (), s32[]{:S(2)}) async-start(), calls=%async_computation.13 | async-start | bytes 17301504 | tf_op jit(solution)/shard_map/reduce_scatter | solution.py:265
  590.5 502.8 %reduce-scatter.9.cloned.1.call-start = ((), (), s32[]{:S(2)}) async-start(), calls=%async_computation.11 | async-start | bytes 17301504 | tf_op jit(solution)/shard_map/reduce_scatter | solution.py:263
  604.5 634.3 %reduce-scatter.7.cloned.1.call-start = ((), (), s32[]{:S(2)}) async-start(), calls=%async_computation.10 | async-start | bytes 4325376 | tf_op jit(solution)/shard_map/reduce_scatter | solution.py:259
  610.1 110.0 %copy-start.99 = (u32[32]{0:T(128)S(1)}, u32[32]{0:T(128)}, u32[]{:S(2)}) copy-start(u32[32]{0:T(128)} %constant.285) | copy-start | bytes 388
  610.1 112.5 %copy-start.98 = (u32[32]{0:T(128)S(1)}, u32[32]{0:T(128)}, u32[]{:S(2)}) copy-start(u32[32]{0:T(128)} %constant.250) | copy-start | bytes 388
  610.1 114.4 %copy-start.74 = (f32[128]{0:T(128)S(1)}, f32[128]{0:T(128)}, u32[]{:S(2)}) copy-start(f32[128]{0:T(128)} %param.43) | copy-start | bytes 1540
  610.1 645.9 %all-gather.29.cloned.1.call-start = ((), (), s32[]{:S(2)}) async-start(), calls=%async_computation.9 | async-start | bytes 1966080 | tf_op jit(solution)/shard_map/all_gather | solution.py:271
  720.0 560.2 %all-gather.33.cloned.1.call-start = ((), (), s32[]{:S(2)}) async-start(), calls=%async_computation.14 | async-start | bytes 2621440 | tf_op jit(solution)/shard_map/all_gather | solution.py:279
  733.5 170.9 %copy-start.81 = (f32[8]{0:T(128)}, f32[8]{0:T(128)S(1)}, u32[]{:S(2)}) copy-start(f32[8]{0:T(128)S(1)} %dynamic-update-slice.15) | copy-start | bytes 100
  734.9 178.5 %copy-start.82 = (f32[8]{0:T(128)}, f32[8]{0:T(128)S(1)}, u32[]{:S(2)}) copy-start(f32[8]{0:T(128)S(1)} %dynamic-update-slice.16) | copy-start | bytes 100
  736.3 168.0 %copy-start.75 = (f32[8]{0:T(128)}, f32[8]{0:T(128)S(1)}, u32[]{:S(2)}) copy-start(f32[8]{0:T(128)S(1)} %dynamic-update-slice.17) | copy-start | bytes 100
  904.4 400.0 %all-gather.31.cloned.1.call-start = ((), (), s32[]{:S(2)}) async-start(), calls=%async_computation.12 | async-start | bytes 2621440 | tf_op jit(solution)/shard_map/all_gather | solution.py:277
  915.8 188.6 %copy-start.67 = (f32[256]{0:T(256)S(1)}, f32[256]{0:T(256)}, u32[]{:S(2)}) copy-start(f32[256]{0:T(256)} %param.54) | copy-start | bytes 3076
  915.8 189.8 %copy-start.68 = (f32[128]{0:T(128)S(1)}, f32[128]{0:T(128)}, u32[]{:S(2)}) copy-start(f32[128]{0:T(128)} %param.53) | copy-start | bytes 1540
  915.8 189.8 %copy-start.69 = (f32[128]{0:T(128)S(1)}, f32[128]{0:T(128)}, u32[]{:S(2)}) copy-start(f32[128]{0:T(128)} %param.52) | copy-start | bytes 1540
  915.8 190.9 %copy-start.70 = (f32[128]{0:T(128)S(1)}, f32[128]{0:T(128)}, u32[]{:S(2)}) copy-start(f32[128]{0:T(128)} %param.56) | copy-start | bytes 1540
  915.8 190.9 %copy-start.71 = (f32[128]{0:T(128)S(1)}, f32[128]{0:T(128)}, u32[]{:S(2)}) copy-start(f32[128]{0:T(128)} %param.55) | copy-start | bytes 1540
  915.8 192.0 %copy-start.72 = (f32[128]{0:T(128)S(1)}, f32[128]{0:T(128)}, u32[]{:S(2)}) copy-start(f32[128]{0:T(128)} %param.59) | copy-start | bytes 1540
  915.8 192.0 %copy-start.73 = (f32[128]{0:T(128)S(1)}, f32[128]{0:T(128)}, u32[]{:S(2)}) copy-start(f32[128]{0:T(128)} %param.57) | copy-start | bytes 1540
  915.8 193.2 %copy-start.55 = (f32[512]{0:T(512)S(1)}, f32[512]{0:T(512)}, u32[]{:S(2)}) copy-start(f32[512]{0:T(512)} %param.58) | copy-start | bytes 6148
  918.0 327.7 %copy-start.83 = (f32[128]{0:T(128)S(1)}, f32[128]{0:T(128)}, u32[]{:S(2)}) copy-start(f32[128]{0:T(128)} %param.46) | copy-start | bytes 1540
  1093.4 284.7 %all-reduce.35.cloned.1.call-start = ((), (), s32[]{:S(2)}) async-start(), calls=%async_computation.15 | async-start | bytes 147456
  1110.3 148.6 %copy-start.84 = (f32[128]{0:T(128)S(1)}, f32[128]{0:T(128)}, u32[]{:S(2)}) copy-start(f32[128]{0:T(128)} %param.44) | copy-start | bytes 1540
  1245.7 295.5 %copy-start.15 = (f32[128,1024]{1,0:T(8,128)}, f32[128,1024]{1,0:T(8,128)S(1)}, u32[]{:S(2)}) copy-start(f32[128,1024]{1,0:T(8,128)S(1)} %get-tuple-element.164) | copy-start | bytes 1572868
  1246.3 140.3 %copy-start.45 = (f32[128]{0:T(128)}, f32[128]{0:T(128)S(1)}, u32[]{:S(2)}) copy-start(f32[128]{0:T(128)S(1)} %get-tuple-element.163) | copy-start | bytes 1540
  1261.7 45.9 %copy-start.20 = (f32[24592]{0:T(1024)}, f32[24592]{0:T(1024)S(1)}, u32[]{:S(2)}) copy-start(f32[24592]{0:T(1024)S(1)} %dynamic-update-slice.7) | copy-start | bytes 295108
  1284.0 263.9 %copy-start.38 = (f32[512]{0:T(512)}, f32[512]{0:T(512)S(1)}, u32[]{:S(2)}) copy-start(f32[512]{0:T(512)S(1)} %get-tuple-element.160) | copy-start | bytes 6148
  1286.3 94.8 %copy-start.53 = (f32[1024]{0:T(1024)S(1)}, f32[1024]{0:T(1024)}, u32[]{:S(2)}) copy-start(f32[1024]{0:T(1024)} %param.51) | copy-start | bytes 12292
  1286.3 94.8 %copy-start.54 = (f32[1024]{0:T(1024)S(1)}, f32[1024]{0:T(1024)}, u32[]{:S(2)}) copy-start(f32[1024]{0:T(1024)} %param.47) | copy-start | bytes 12292
  1286.3 167.3 %all-reduce.37.cloned.1.call-start = ((), (), s32[]{:S(2)}) async-start(), calls=%async_computation.16 | async-start | bytes 475136
  1381.1 160.0 %copy-start.34 = (f32[1024]{0:T(1024)}, f32[1024]{0:T(1024)S(1)}, u32[]{:S(2)}) copy-start(f32[1024]{0:T(1024)S(1)} %get-tuple-element.234) | copy-start | bytes 12292
  1381.1 166.8 %copy-start.37 = (f32[1024]{0:T(1024)}, f32[1024]{0:T(1024)S(1)}, u32[]{:S(2)}) copy-start(f32[1024]{0:T(1024)S(1)} %get-tuple-element.233) | copy-start | bytes 12292
  1453.6 87.5 %copy-start.17 = (f32[128,1024]{1,0:T(8,128)S(1)}, f32[128,1024]{1,0:T(8,128)}, u32[]{:S(2)}) copy-start(f32[128,1024]{1,0:T(8,128)} %param.36) | copy-start | bytes 1572868
  1458.8 84.0 %copy-start.27 = (f32[3072]{0:T(1024)}, f32[3072]{0:T(1024)S(1)}, u32[]{:S(2)}) copy-start(f32[3072]{0:T(1024)S(1)} %fusion.63) | copy-start | bytes 36868
  1464.0 81.9 %copy-start.24 = (f32[4096]{0:T(1024)}, f32[4096]{0:T(1024)S(1)}, u32[]{:S(2)}) copy-start(f32[4096]{0:T(1024)S(1)} %fusion.62) | copy-start | bytes 49156
  1464.1 78.8 %copy-start.44 = (f32[128]{0:T(128)S(1)}, f32[128]{0:T(128)}, u32[]{:S(2)}) copy-start(f32[128]{0:T(128)} %get-tuple-element.169) | copy-start | bytes 1540
  (65 other events, 544.6 us)
Sparse Core Ops, SparseCore 0:
  11.3 101.9 all-gather.20
  116.0 47.6 all-gather.22
  166.4 123.4 all-gather.24
  292.4 123.0 all-gather.26
  566.4 153.5 reduce-scatter.4
  722.2 182.1 reduce-scatter.10
  906.8 186.5 reduce-scatter.8
  1095.7 143.0 reduce-scatter.6
  1240.4 15.5 all-gather.28
  1257.5 22.5 all-gather.32
  1281.8 22.5 all-gather.30
  1309.3 68.6 all-reduce.34
  1383.0 70.6 all-reduce.36
